TPU v7x, 256 devices: a whole 4x4x8 slice. The times are simulated.
256 devices in a mesh: row: 16 (over x_lo, y, core), col: 16 (over z, x_hi).
Axes of the slice: x: 4 (x_hi: 2, x_lo: 2; x = x_hi * 2 + x_lo), y: 4, z: 8, core: 2. Of those that a mesh axis runs over, the one named last changes fastest.
Arguments:
- green: bfloat16 [32768, 32768], P('row', 'col'), may hold values from -0.046875 to 0.046875
- mask: int32 [128, 128], P('row', 'col'), may hold values from 0 to 1, as said below
- probes: bfloat16 [32768, 256], P('col', 'row'), may hold values from -6 to 6
Outputs:
- sketch: float32 [32768, 256], P('row', 'col')
- adjoint: float32 [32768, 256], P('col', 'row')
Inputs may be any that keep to these rules, and one draw needn't show every extreme that they name: `mask`: block row i belongs to gauge i % 6 and time block i // 6; block column j to window j // 8. A block is 1 when its time block is no earlier than the window's onset plus a travel delay of its gauge and subfault block.
All inputs are finite; a program needn't handle non-finite values.
Results may differ from a plain program's by a relative error of at most 0.0022.
Values may be sent and summed in bfloat16 or wider, within the bound.
A program may use at most 128 MiB of HBM per device.

v0:
```python
import jax
import jax.numpy as jnp
from jax import lax
from jax.sharding import PartitionSpec as P


def local(green, mask, probes):
    row_blocks, col_blocks = mask.shape
    block_size = green.shape[0] // row_blocks
    shaped = green.reshape(row_blocks, block_size, col_blocks, block_size)
    tiles = (shaped * mask.astype(jnp.bfloat16)[:, None, :, None]).reshape(green.shape)
    partial_sketch = jnp.dot(
        tiles, lax.all_gather(probes, "row", axis=1, tiled=True), preferred_element_type=jnp.float32
    )
    summed = lax.psum(partial_sketch, "col")
    width_own = summed.shape[1] // lax.axis_size("col")
    own_sketch = lax.dynamic_slice_in_dim(summed, lax.axis_index("col") * width_own, width_own, 1)
    term = lax.dot_general(
        tiles,
        summed.astype(jnp.bfloat16),
        (((0,), (0,)), ((), ())),
        preferred_element_type=jnp.float32,
    )
    adjoint = lax.psum_scatter(term, "row", scatter_dimension=1, tiled=True)
    return (own_sketch, adjoint)


def solution(mesh):
    in_specs = (P("row", "col"), P("row", "col"), P("col", "row"))
    out_specs = (P("row", "col"), P("col", "row"))
    return jax.shard_map(local, mesh=mesh, in_specs=in_specs, out_specs=out_specs, check_vma=False)
```

profile of v0, /device:TPU:32, one launch (start us, length us, event | category | flops | bytes accessed | tf_op | source)
XLA Modules:
  0.0 299.5 jit_solution(3500955319090247931)
XLA Ops:
  7.2 0.0 all-gather.2.cloned.1.call-start
  7.2 0.7 all-gather.2.cloned.1.call-update
  7.9 0.0 all-reduce.2.cloned.1.call-start
  7.9 0.7 convert_element_type.6
  8.6 3.8 %mul.14 = bf16[8,256,8,256]{3,2,1,0:T(8,128)(2,1)} broadcast(bf16[8,8]{1,0:T(8,128)(2,1)S(1)} %convert_element_type.6), dimensions={0,2} | broadcast | bytes 8388736 | tf_op jit(solution)/shard_map/mul | solution.py:11
  12.5 10.3 %copy.6 = bf16[256,8,8,256]{3,1,2,0:T(8,128)(2,1)} copy(bf16[256,8,8,256]{3,2,1,0:T(8,128)(2,1)} %bitcast.7) | data formatting | bytes 16777216
  22.7 10.5 %mul.16 = bf16[2048,2048]{1,0:T(8,128)(2,1)} multiply(bf16[2048,2048]{1,0:T(8,128)(2,1)} %param.3, bf16[2048,2048]{1,0:T(8,128)(2,1)} %bitcast.6) | non-fusion elementwise | flops 4194304 | bytes 25165824 | tf_op jit(solution)/shard_map/mul | solution.py:11
  33.3 14.2 %all-gather.2.cloned.1.call-done = bf16[2048,256]{0,1:T(8,128)(2,1)} async-done(((bf16[2048,16]{0,1:T(8,128)(2,1)}), bf16[2048,256]{0,1:T(8,128)(2,1)}) %all-gather.2.cloned.1.call-update) | async-done | bytes 1048592 | tf_op jit(solution)/shard_map/all_gather | solution.py:13
  47.5 7.3 %fusion.2 = f32[2048,256]{1,0:T(8,128)} fusion(bf16[2048,2048]{1,0:T(8,128)(2,1)} %mul.16, bf16[2048,256]{0,1:T(8,128)(2,1)} %all-gather.2.cloned.1.call-done), kind=kOutput, calls=%fused_computation.3 | convolution fusion | flops 2147483648 | bytes 11534336 | tf_op jit(solution)/shard_map/dot_general | solution.py:12
  54.8 0.0 all-reduce.2.cloned.1.call-update
  54.8 0.0 reduce-scatter.2.cloned.1.call-start
  54.9 166.0 %all-reduce.2.cloned.1.call-done = f32[2048,256]{1,0:T(8,128)} async-done(((f32[2048,256]{1,0:T(8,128)}), f32[2048,256]{1,0:T(8,128)}) %all-reduce.2.cloned.1.call-update) | async-done | bytes 2097168 | tf_op jit(solution)/shard_map/psum | solution.py:15
  220.9 0.0 copy-start
  220.9 7.8 %fusion = f32[2048,256]{0,1:T(8,128)} fusion(bf16[2048,2048]{1,0:T(8,128)(2,1)} %mul.16, f32[2048,256]{1,0:T(8,128)} %all-reduce.2.cloned.1.call-done), kind=kOutput, calls=%fused_computation | convolution fusion | flops 2148007936 | bytes 12582912 | tf_op jit(solution)/shard_map/dot_general | solution.py:18
  228.7 0.0 reduce-scatter.2.cloned.1.call-update
  228.7 0.0 copy-done
  228.7 0.3 constant_dynamic-slice_fusion
  229.1 1.0 copy.5
  230.0 62.9 %reduce-scatter.2.cloned.1.call-done = f32[2048,16]{0,1:T(8,128)} async-done(((f32[2048,256]{0,1:T(8,128)}), f32[2048,16]{0,1:T(8,128)}) %reduce-scatter.2.cloned.1.call-update) | async-done | bytes 131088 | tf_op jit(solution)/shard_map/reduce_scatter | solution.py:24
Async XLA Ops:
  7.2 40.3 %all-gather.2.cloned.1.call-start = ((), (), s32[]{:S(2)}) async-start(), calls=%async_computation.1 | async-start | bytes 1114112 | tf_op jit(solution)/shard_map/all_gather | solution.py:13
  7.9 213.0 %all-reduce.2.cloned.1.call-start = ((), (), s32[]{:S(2)}) async-start(), calls=%async_computation.2 | async-start | bytes 4194304 | tf_op jit(solution)/shard_map/psum | solution.py:15
  54.8 238.2 %reduce-scatter.2.cloned.1.call-start = ((), (), s32[]{:S(2)}) async-start(), calls=%async_computation.3 | async-start | bytes 2228224 | tf_op jit(solution)/shard_map/reduce_scatter | solution.py:24
  220.9 7.8 %copy-start = (f32[2048,256]{1,0:T(8,128)S(1)}, f32[2048,256]{1,0:T(8,128)}, u32[]{:S(2)}) copy-start(f32[2048,256]{1,0:T(8,128)} %all-reduce.2.cloned.1.call-done) | copy-start | bytes 6291460
Sparse Core Ops, SparseCore 0:
  9.8 37.5 all-gather.1
  54.9 165.8 all-reduce.1
  228.8 64.0 reduce-scatter.1
where the time goes:
time: 300 us
  waiting for transfers between devices  244 us (81%)
  local copies, waits for them, and re-layouts  15.4 us (5%)
  matrix products  15.1 us (5%)
  between operations  13.8 us (5%)
  other arithmetic  11.2 us (4%)
    psum x1, waiting for transfers between devices, local(): summed = lax.psum(partial_sketch, 'col')  166 us
    reduce_scatter x1, waiting for transfers between devices, local(): adjoint = lax.psum_scatter(term, 'row', scatter_dimension=1, tiled=True)  62.9 us
    all_gather x1, waiting for transfers between devices, local(): lax.all_gather(probes, 'row', axis=1, tiled=True)  14.2 us
    unnamed x4, local copies, waits for them, and re-layouts  11.2 us
    mul x1, other arithmetic, local(): shaped * mask.astype(jnp.bfloat16)[:, None, :, None]  10.5 us
    dot_general x1, matrix products, local(): lax.dot_general(tiles, summed.astype(jnp.bfloat16), (((0,), (0,)), ((), (...  7.8 us
    dot_general x1, matrix products, local(): jnp.dot(tiles, lax.all_gather(probes, 'row', axis=1, tiled=True), preferr...  7.31 us
  transfers between devices with their start and end apart: 3, of which 3 were waited for; matrix products, arithmetic and copies ran while one was open for 9% of the time, Pallas kernels for 0%

commit v1 on v0

--- a/solution.py
+++ b/solution.py
@@ -12,7 +12,7 @@
     partial_sketch = jnp.dot(
         tiles, lax.all_gather(probes, "row", axis=1, tiled=True), preferred_element_type=jnp.float32
     )
-    summed = lax.psum(partial_sketch, "col")
+    summed = jnp.sum(lax.all_gather(partial_sketch, "col"), axis=0)
     width_own = summed.shape[1] // lax.axis_size("col")
     own_sketch = lax.dynamic_slice_in_dim(summed, lax.axis_index("col") * width_own, width_own, 1)
     term = lax.dot_general(

time: 300 us -> 557 us (1.86)
  waiting for transfers between devices: 244 us -> 490 us
  other arithmetic: 11.2 us -> 23.3 us
    all_gather x0 -> x1, waiting for transfers between devices: none -> 412 us  [local(): summed = jnp.sum(lax.all_gather(partial_sketch, 'col'), axis=0)]
    psum x1 -> x0, waiting for transfers between devices: 166 us -> none  [local(): summed = lax.psum(partial_sketch, 'col')]
    reduce_sum x0 -> x1, other arithmetic: none -> 12.1 us  [local(): summed = jnp.sum(lax.all_gather(partial_sketch, 'col'), axis=0)]
    unnamed x4 -> x2, local copies, waits for them, and re-layouts: 11.2 us -> 11.2 us
  transfers between devices with their start and end apart: 3 -> 3, of which waited for: 3 -> 3; matrix products, arithmetic and copies ran while one was open for 9% -> 5% of each run, Pallas kernels for 0% -> 0%
where the time goes in v1:
time: 557 us
  waiting for transfers between devices  490 us (88%)
  other arithmetic  23.3 us (4%)
  local copies, waits for them, and re-layouts  15.4 us (3%)
  matrix products  14.4 us (3%)
  between operations  13.8 us (2%)
    all_gather x1, waiting for transfers between devices, local(): summed = jnp.sum(lax.all_gather(partial_sketch, 'col'), axis=0)  412 us
    reduce_scatter x1, waiting for transfers between devices, local(): adjoint = lax.psum_scatter(term, 'row', scatter_dimension=1, tiled=True)  63.3 us
    all_gather x1, waiting for transfers between devices, local(): lax.all_gather(probes, 'row', axis=1, tiled=True)  14.2 us
    reduce_sum x1, other arithmetic, local(): summed = jnp.sum(lax.all_gather(partial_sketch, 'col'), axis=0)  12.1 us
    unnamed x2, local copies, waits for them, and re-layouts  11.2 us
  transfers between devices with their start and end apart: 3, of which 3 were waited for; matrix products, arithmetic and copies ran while one was open for 5% of the time, Pallas kernels for 0%

profile of v1, /device:TPU:32, one launch (start us, length us, event | category | flops | bytes accessed | tf_op | source)
XLA Modules:
  0.0 556.8 jit_solution(11488618515080273063)
XLA Ops:
  7.2 0.0 all-gather.4.cloned.1.call-start
  7.2 0.7 all-gather.4.cloned.1.call-update
  7.9 0.0 all-gather.6.cloned.1.call-start
  7.9 0.7 convert_element_type.6
  8.6 3.8 mul.14
  12.5 10.3 %copy.6 = bf16[256,8,8,256]{3,1,2,0:T(8,128)(2,1)} copy(bf16[256,8,8,256]{3,2,1,0:T(8,128)(2,1)} %bitcast.9) | data formatting | bytes 16777216
  22.7 10.5 %mul.16 = bf16[2048,2048]{1,0:T(8,128)(2,1)} multiply(bf16[2048,2048]{1,0:T(8,128)(2,1)} %param.3, bf16[2048,2048]{1,0:T(8,128)(2,1)} %bitcast.7) | non-fusion elementwise | flops 4194304 | bytes 25165824 | tf_op jit(solution)/shard_map/mul | solution.py:11
  33.2 14.2 %all-gather.4.cloned.1.call-done = bf16[2048,256]{0,1:T(8,128)(2,1)} async-done(((bf16[2048,16]{0,1:T(8,128)(2,1)}), bf16[2048,256]{0,1:T(8,128)(2,1)}) %all-gather.4.cloned.1.call-update) | async-done | bytes 1048592 | tf_op jit(solution)/shard_map/all_gather | solution.py:13
  47.5 7.4 %fusion.2 = f32[2048,256]{1,0:T(8,128)} fusion(bf16[2048,2048]{1,0:T(8,128)(2,1)} %mul.16, bf16[2048,256]{0,1:T(8,128)(2,1)} %all-gather.4.cloned.1.call-done), kind=kOutput, calls=%fused_computation.3 | convolution fusion | flops 2147483648 | bytes 11534336 | tf_op jit(solution)/shard_map/dot_general | solution.py:12
  54.8 0.0 all-gather.6.cloned.1.call-update
  54.9 0.0 reduce-scatter.2.cloned.1.call-start
  54.9 411.5 %all-gather.6.cloned.1.call-done = f32[32768,256]{1,0:T(8,128)} async-done(((f32[2048,256]{1,0:T(8,128)}), f32[32768,256]{1,0:T(8,128)}) %all-gather.6.cloned.1.call-update) | async-done | bytes 33554448 | tf_op jit(solution)/shard_map/all_gather | solution.py:15
  466.4 12.1 %reduce_sum.9 = f32[2048,256]{1,0:T(8,128)S(1)} reduce(f32[16,2048,256]{2,1,0:T(8,128)} %bitcast.8, f32[]{:T(128)} %constant.5.clone.1), dimensions={0}, to_apply=%region_0.0 | reduce | flops 7864320 | bytes 35651588 | tf_op jit(solution)/shard_map/reduce_sum | solution.py:15
  478.5 7.1 %fusion = f32[2048,256]{0,1:T(8,128)} fusion(bf16[2048,2048]{1,0:T(8,128)(2,1)} %mul.16, f32[2048,256]{1,0:T(8,128)S(1)} %reduce_sum.9), kind=kOutput, calls=%fused_computation | convolution fusion | flops 2148007936 | bytes 12582912 | tf_op jit(solution)/shard_map/dot_general | solution.py:18
  485.6 0.0 reduce-scatter.2.cloned.1.call-update
  485.6 0.3 constant_dynamic-slice_fusion
  486.0 1.0 copy.5
  486.9 63.3 %reduce-scatter.2.cloned.1.call-done = f32[2048,16]{0,1:T(8,128)} async-done(((f32[2048,256]{0,1:T(8,128)}), f32[2048,16]{0,1:T(8,128)}) %reduce-scatter.2.cloned.1.call-update) | async-done | bytes 131088 | tf_op jit(solution)/shard_map/reduce_scatter | solution.py:24
Async XLA Ops:
  7.2 40.3 %all-gather.4.cloned.1.call-start = ((), (), s32[]{:S(2)}) async-start(), calls=%async_computation.1 | async-start | bytes 1114112 | tf_op jit(solution)/shard_map/all_gather | solution.py:13
  7.9 458.5 %all-gather.6.cloned.1.call-start = ((), (), s32[]{:S(2)}) async-start(), calls=%async_computation.3 | async-start | bytes 35651584 | tf_op jit(solution)/shard_map/all_gather | solution.py:15
  54.9 495.4 %reduce-scatter.2.cloned.1.call-start = ((), (), s32[]{:S(2)}) async-start(), calls=%async_computation.2 | async-start | bytes 2228224 | tf_op jit(solution)/shard_map/reduce_scatter | solution.py:24
Sparse Core Ops, SparseCore 0:
  9.8 37.5 all-gather.3
  55.0 411.3 all-gather.5
  485.7 64.4 reduce-scatter.1
